TPU v7x, 512 devices: a whole 4x4x16 slice. The times are simulated.
512 devices in a mesh: scen: 32 (over z, core), row: 16 (over x, y).
Axes of the slice: x: 4, y: 4, z: 16, core: 2. Of those that a mesh axis runs over, the one named last changes fastest.
Arguments:
- coupling: bfloat16 [32, 1536, 16384], P('scen', None, 'row'), may hold values from -40 to 40
- solves: bfloat16 [32, 1536, 512], P('scen', 'row'), may hold values from -0.625 to 0.625
- border_diagonal: float32 [1024, 16], P('scen', 'row'), may hold values from 32 to 64
- panel_rows: int32 [512], replicated, may hold values from 0 to 16383, as said below
Outputs:
- first_factor: float32 [1024, 16, 256], P('scen', 'row')
- second_factor: float32 [1024, 16, 256], P('scen', 'row')
Inputs may be any that keep to these rules, and one draw needn't show every extreme that they name: `panel_rows`: 512 distinct border rows; the first 256 are the first panel's pivot rows and columns, the rest the second's.
All inputs are finite; a program needn't handle non-finite values. Where the computation divides by a largest or mean magnitude, that divisor is 1e-20 or more.
Results may differ from a plain program's by a relative error of at most 0.0003.
Values may be sent and summed in bfloat16 or wider, within the bound.
A program may use at most 64 MiB of HBM per device.

v0:
```python
import jax
import jax.numpy as jnp
from jax import lax
from jax.sharding import PartitionSpec as P

HALF = 256
NEWTON = 8


def pick_rows(local, panel_rows, base):
    offset = panel_rows - base
    owned = (offset >= 0) & (offset < local.shape[0])
    taken = jnp.take(local, jnp.clip(offset, 0, local.shape[0] - 1), axis=0)
    return jnp.where(owned[:, None], taken, jnp.float32(0.0))


def newton_start(pivot):
    norm_one = jnp.max(jnp.sum(jnp.abs(pivot), axis=0))
    norm_inf = jnp.max(jnp.sum(jnp.abs(pivot), axis=1))
    return pivot.T / (norm_one * norm_inf)


def invert(pivot):
    start_guess = newton_start(pivot)
    approx = start_guess
    for step in range(NEWTON):
        left = jnp.dot(approx, pivot, precision=lax.Precision.HIGHEST)
        approx = 2.0 * approx - jnp.dot(left, approx, precision=lax.Precision.HIGHEST)
    return approx


def shards(coupling, solves, border_diagonal, panel_rows):
    half_cols = HALF
    full_solves = lax.all_gather(solves, "row", axis=1, tiled=True)
    row_count = coupling.shape[2]
    share = row_count // lax.axis_size("scen")
    base = lax.axis_index("row") * row_count + lax.axis_index("scen") * share
    glob = base + jnp.arange(share, dtype=jnp.int32)
    diag_part = jnp.where(
        glob[:, None] == panel_rows[None, :], border_diagonal[:, 0][:, None], jnp.float32(0.0)
    )
    both = (
        lax.psum_scatter(
            jnp.einsum("snr,snc->rc", coupling, full_solves, preferred_element_type=jnp.float32),
            "scen",
            scatter_dimension=0,
            tiled=True,
        )
        + diag_part
    )
    pivots = lax.psum(pick_rows(both, panel_rows, base), ("scen", "row"))
    first = both[:, :half_cols]
    second = both[:, half_cols:]
    pivots_first = pivots[:, :half_cols]
    pivots_second = pivots[:, half_cols:]
    inverse_first = invert(pivots_first[:half_cols])
    first_factor = jnp.dot(first, inverse_first, precision=lax.Precision.HIGHEST)
    upper = pivots_second[:half_cols]
    updated = second - jnp.dot(first_factor, upper, precision=lax.Precision.HIGHEST)
    lower_factor = jnp.dot(pivots_first[half_cols:], inverse_first, precision=lax.Precision.HIGHEST)
    pivot_two = pivots_second[half_cols:] - jnp.dot(
        lower_factor, upper, precision=lax.Precision.HIGHEST
    )
    inverse_second = invert(pivot_two)
    second_factor = jnp.dot(updated, inverse_second, precision=lax.Precision.HIGHEST)
    return (first_factor[:, None, :], second_factor[:, None, :])


def solution(mesh):
    placed = (P("scen", None, "row"), P("scen", "row", None), P("scen", "row"), P())
    return jax.shard_map(
        shards,
        mesh=mesh,
        in_specs=placed,
        out_specs=(P("scen", "row", None), P("scen", "row", None)),
        check_vma=False,
    )
```

profile of v0, /device:TPU:1, one launch (start us, length us, event | category | flops | bytes accessed | tf_op | source)
XLA Modules:
  0.0 703.2 jit_solution(12744666268272097158)
XLA Ops:
  7.2 0.7 all-gather.2.cloned.1.call-update
  8.0 66.1 %all-gather.2.cloned.1.call-done = bf16[1,1536,512]{2,1,0:T(8,128)(2,1)} async-done(((bf16[1,96,512]{2,1,0:T(8,128)(2,1)}), bf16[1,1536,512]{2,1,0:T(8,128)(2,1)}) %all-gather.2.cloned.1.call-update) | async-done | bytes 1572880 | tf_op jit(solution)/shard_map/all_gather | solution.py:34
  74.1 4.6 fusion
  78.8 0.6 copy-done.2
  79.4 108.8 %reduce-scatter.2.cloned.1.call-done = f32[32,512]{1,0:T(8,128)} async-done(((f32[1024,512]{1,0:T(8,128)}), f32[32,512]{1,0:T(8,128)}) %reduce-scatter.2.cloned.1.call-update) | async-done | bytes 65552 | tf_op jit(solution)/shard_map/reduce_scatter | solution.py:43
  188.2 0.9 select_add_fusion
  189.1 2.3 gather_fusion
  191.4 2.6 copy.6
  194.0 2.4 select_select_fusion
  196.4 474.6 %all-reduce.2.cloned.1.call-done = f32[512,512]{0,1:T(8,128)} async-done(((f32[512,512]{0,1:T(8,128)}), f32[512,512]{0,1:T(8,128)}) %all-reduce.2.cloned.1.call-update) | async-done | bytes 1048592 | tf_op jit(solution)/shard_map/psum | solution.py:51
  671.0 1.1 abs_reduce_fusion.2
  672.1 0.6 reduce_max.36
  672.7 0.6 reduce_max.37
  674.6 1.5 fusion.10
  676.1 1.4 convolution_subtract_fusion.16
  677.6 0.4 fusion.29
  680.0 0.4 fusion.23
  681.6 0.4 fusion.19
  682.4 0.4 fusion.17
  683.5 0.6 copy.10
  684.1 0.6 fusion.3
  684.7 0.5 abs_reduce_fusion
  685.2 0.6 reduce_max.38
  685.8 0.7 reduce_max.39
  687.8 0.4 fusion.7
  688.7 0.4 fusion.35
  690.3 0.4 fusion.37
  691.1 0.4 fusion.38
  691.9 0.6 fusion.39
  693.7 0.4 fusion.41
  694.5 1.3 convolution_subtract_fusion.17
  696.1 0.6 copy.11
  (37 shorter events, 8.4 us)
Async XLA Ops:
  7.2 66.9 %copy-start = (bf16[1,1536,1024]{2,1,0:T(8,128)(2,1)S(1)}, bf16[1,1536,1024]{2,1,0:T(8,128)(2,1)}, u32[]{:S(2)}) copy-start(bf16[1,1536,1024]{2,1,0:T(8,128)(2,1)} %param.4) | copy-start | bytes 9437188
  7.2 66.9 %all-gather.2.cloned.1.call-start = ((), (), s32[]{:S(2)}) async-start(), calls=%async_computation.1 | async-start | bytes 1671168 | tf_op jit(solution)/shard_map/all_gather | solution.py:34
  7.9 180.3 %reduce-scatter.2.cloned.1.call-start = ((), (), s32[]{:S(2)}) async-start(), calls=%async_computation.2 | async-start | bytes 2162688 | tf_op jit(solution)/shard_map/reduce_scatter | solution.py:43
  78.7 0.7 copy-start.2
  78.7 109.5 %copy-start.3 = (f32[32,1]{0,1:T(1,128)S(1)}, f32[32,1]{0,1:T(1,128)}, u32[]{:S(2)}) copy-start(f32[32,1]{0,1:T(1,128)} %param.6) | copy-start | bytes 388
  78.7 592.3 %all-reduce.2.cloned.1.call-start = ((), (), s32[]{:S(2)}) async-start(), calls=%async_computation.3 | async-start | bytes 2097152 | tf_op jit(solution)/shard_map/psum | solution.py:51
  674.6 3.0 copy-start.1
Sparse Core Ops, SparseCore 0:
  11.0 62.9 all-gather.1
  78.8 109.3 reduce-scatter.1
  196.6 474.4 all-reduce.1
where the time goes:
time: 704 us; the launch traced here: 703 us
  waiting for transfers between devices  650 us (92%)
  matrix products  22.5 us (3%)
  between operations  16.7 us (2%)
    psum x1, waiting for transfers between devices, shards(): pivots = lax.psum(pick_rows(both, panel_rows, base), ('scen', 'row'))  475 us
    reduce_scatter x1, waiting for transfers between devices, shards(): lax.psum_scatter(jnp.einsum('snr,snc->rc', coupling, full_solves, preferr...  109 us
    all_gather x1, waiting for transfers between devices, shards(): full_solves = lax.all_gather(solves, 'row', axis=1, tiled=True)  66.1 us
  transfers between devices with their start and end apart: 3, of which 3 were waited for; matrix products, arithmetic and copies ran while one was open for 0% of the time, Pallas kernels for 0%

commit v1 on v0

v1 whole, which is shorter than its diff:
```python
import jax
import jax.numpy as jnp
from jax import lax
from jax.sharding import PartitionSpec as P

HALF = 256
NEWTON = 8


def newton_start(pivot):
    norm_one = jnp.max(jnp.sum(jnp.abs(pivot), axis=0))
    norm_inf = jnp.max(jnp.sum(jnp.abs(pivot), axis=1))
    return pivot.T / (norm_one * norm_inf)


def invert(pivot):
    approx = newton_start(pivot)
    for step in range(NEWTON):
        left = jnp.dot(approx, pivot, precision=lax.Precision.HIGHEST)
        approx = 2.0 * approx - jnp.dot(left, approx, precision=lax.Precision.HIGHEST)
    return approx


def eliminate(both, pivots):
    first = both[:, :HALF]
    second = both[:, HALF:]
    inverse_first = invert(pivots[:HALF, :HALF])
    first_factor = jnp.dot(first, inverse_first, precision=lax.Precision.HIGHEST)
    upper = pivots[:HALF, HALF:]
    updated = second - jnp.dot(first_factor, upper, precision=lax.Precision.HIGHEST)
    lower_factor = jnp.dot(pivots[HALF:, :HALF], inverse_first, precision=lax.Precision.HIGHEST)
    pivot_two = pivots[HALF:, HALF:] - jnp.dot(
        lower_factor, upper, precision=lax.Precision.HIGHEST
    )
    inverse_second = invert(pivot_two)
    second_factor = jnp.dot(updated, inverse_second, precision=lax.Precision.HIGHEST)
    return (first_factor[:, None, :], second_factor[:, None, :])


def shards(coupling, solves, border_diagonal, panel_rows):
    scens = lax.axis_size("scen")
    full_solves = lax.all_gather(solves[0], "row", axis=0, tiled=True)
    row_count = coupling.shape[2]
    panel = panel_rows.shape[0]
    share = row_count // scens
    pivot_share = panel // scens
    first_row = lax.axis_index("row") * row_count
    base = first_row + lax.axis_index("scen") * share
    local = first_row + jnp.arange(row_count, dtype=jnp.int32)
    pick = (local[:, None] == panel_rows[None, :]).astype(jnp.bfloat16)
    chosen = jnp.dot(coupling[0], pick, preferred_element_type=jnp.float32).astype(jnp.bfloat16)
    glob = base + jnp.arange(share, dtype=jnp.int32)
    diag_part = jnp.where(
        glob[:, None] == panel_rows[None, :], border_diagonal[:, 0][:, None], jnp.float32(0.0)
    )
    main = jnp.einsum("nr,nc->rc", coupling[0], full_solves, preferred_element_type=jnp.float32)
    extra = jnp.einsum("nr,nc->rc", chosen, full_solves, preferred_element_type=jnp.float32)
    diag_row = jnp.sum(diag_part, axis=0)
    order = jnp.arange(panel, dtype=jnp.int32)
    extra = extra + jnp.where(order[:, None] == order[None, :], diag_row[:, None], jnp.float32(0.0))
    joined = jnp.concatenate(
        [main.reshape(scens, share, panel), extra.reshape(scens, pivot_share, panel)], axis=1
    ).reshape(scens * (share + pivot_share), panel)
    summed = lax.psum_scatter(joined, "scen", scatter_dimension=0, tiled=True)
    both = summed[:share] + diag_part
    pivots = lax.all_gather(lax.psum(summed[share:], "row"), "scen", axis=0, tiled=True)
    return eliminate(both, pivots)


def solution(mesh):
    placed = (P("scen", None, "row"), P("scen", "row", None), P("scen", "row"), P())
    return jax.shard_map(
        shards,
        mesh=mesh,
        in_specs=placed,
        out_specs=(P("scen", "row", None), P("scen", "row", None)),
        check_vma=False,
    )
```

time: 704 us -> 380 us (0.54)
  waiting for transfers between devices: 650 us -> 254 us
  blocking collectives: 0 us -> 62.9 us
    psum x1 -> x0, waiting for transfers between devices: 475 us -> none  [shards(): pivots = lax.psum(pick_rows(both, panel_rows, base), ('scen', 'row'))]
    all_gather x1 -> x2, waiting for transfers between devices: 66.1 us -> 142 us  [the longest x1 80.9 us: shards(): lax.all_gather(lax.psum(summed[share:], 'row'), 'scen', axis=0, tiled=True)]
    psum x0 -> x1, blocking collectives: none -> 62.9 us  [shards(): lax.psum(summed[share:], 'row')]
    dot_general x6 -> x7, matrix products: 7.44 us -> 14.2 us  [the longest x1 6.82 us: shards(): jnp.einsum('nr,nc->rc', chosen, full_solves, preferred_element_type=jnp.f...]
  transfers between devices with their start and end apart: 3 -> 3, of which waited for: 3 -> 3; matrix products, arithmetic and copies ran while one was open for 0% -> 1% of each run, Pallas kernels for 0% -> 0%
where the time goes in v1:
time: 380 us; the launch traced here: 379 us
  waiting for transfers between devices  254 us (67%)
  blocking collectives  62.9 us (17%)
  matrix products  27.9 us (7%)
  between operations  16.8 us (4%)
  other arithmetic  9.84 us (3%)
  local copies, waits for them, and re-layouts  7.84 us (2%)
    reduce_scatter x1, waiting for transfers between devices, shards(): summed = lax.psum_scatter(joined, 'scen', scatter_dimension=0, tiled=True)  111 us
    all_gather x1, waiting for transfers between devices, shards(): lax.all_gather(lax.psum(summed[share:], 'row'), 'scen', axis=0, tiled=True)  80.9 us
    psum x1, blocking collectives, shards(): lax.psum(summed[share:], 'row')  62.9 us
    all_gather x1, waiting for transfers between devices, shards(): full_solves = lax.all_gather(solves[0], 'row', axis=0, tiled=True)  61.3 us
  transfers between devices with their start and end apart: 3, of which 3 were waited for; matrix products, arithmetic and copies ran while one was open for 1% of the time, Pallas kernels for 0%

profile of v1, /device:TPU:1, one launch (start us, length us, event | category | flops | bytes accessed | tf_op | source)
XLA Modules:
  0.0 379.4 jit_solution(10972468629215874356)
XLA Ops:
  7.2 0.7 all-gather.6.cloned.1.call-update
  8.0 4.7 %copy.20 = bf16[1,1536,1024]{1,2,0:T(8,128)(2,1)} copy(bf16[1,1536,1024]{2,1,0:T(8,128)(2,1)} %param.4) | data formatting | bytes 6291456 | tf_op args[0]
  12.8 61.3 %all-gather.6.cloned.1.call-done = bf16[1,1536,512]{2,1,0:T(8,128)(2,1)} async-done(((bf16[1,96,512]{2,1,0:T(8,128)(2,1)}), bf16[1,1536,512]{2,1,0:T(8,128)(2,1)}) %all-gather.6.cloned.1.call-update) | async-done | bytes 1572880 | tf_op jit(solution)/shard_map/all_gather | solution.py:42
  74.1 5.6 %fusion.6 = f32[32,32,512]{2,1,0:T(8,128)} fusion(bf16[32,32,1536]{2,1,0:T(8,128)(2,1)} %bitcast.91, bf16[1,1536,512]{2,1,0:T(8,128)(2,1)} %all-gather.6.cloned.1.call-done), kind=kOutput, calls=%fused_computation.5 | convolution fusion | flops 1610612736 | bytes 6815744 | tf_op jit(solution)/shard_map/nr,nc->rc/dot_general | solution.py:56
  79.7 6.8 %fusion.10 = f32[512,512]{1,0:T(8,128)} fusion(bf16[1,1536,512]{2,1,0:T(8,128)(2,1)} %all-gather.6.cloned.1.call-done, bf16[1,1536,1024]{2,1,0:T(8,128)(2,1)S(1)} %copy-done.1, s32[512]{0:T(512)S(1)} %copy-done.2, s32[1024]{0:T(1024)S(1)} %iota_add_fusion, f32[512]{0:T(512)S(1)} %select_reduce_fusion), kind=kOutput, calls=%fused_computation.9 | convolution fusion | flops 2418016256 | bytes 5775360 | tf_op jit(solution)/shard_map/nr,nc->rc/dot_general | solution.py:57
  86.5 4.1 %pad_maximum_fusion = f32[32,48,512]{2,1,0:T(8,128)} fusion(f32[32,16,512]{2,1,0:T(8,128)} %bitcast.92, f32[32,32,512]{2,1,0:T(8,128)} %fusion.6), kind=kLoop, calls=%fused_computation | loop fusion | flops 786432 | bytes 6291456 | tf_op jit(solution)/shard_map/concatenate | solution.py:61
  90.7 111.2 %reduce-scatter.4.cloned.1.call-done = f32[48,512]{1,0:T(8,128)} async-done(((f32[1536,512]{1,0:T(8,128)}), f32[48,512]{1,0:T(8,128)}) %reduce-scatter.4.cloned.1.call-update) | async-done | bytes 98320 | tf_op jit(solution)/shard_map/reduce_scatter | solution.py:64
  201.9 0.8 slice.34
  202.8 62.9 %psum.7 = f32[16,512]{0,1:T(8,128)S(1)} all-reduce(f32[16,512]{0,1:T(8,128)S(1)} %copy.33), channel_id=1, replica_groups=mesh['scen'=32,'row'=16] {'row'}, use_global_device_ids=true, to_apply=%region_2.3 | all-reduce | flops 8192 | bytes 65536 | tf_op jit(solution)/shard_map/psum | solution.py:66
  265.7 0.7 copy.23
  266.4 0.9 select_add_fusion
  267.4 80.9 %all-gather.4.cloned.1.call-done = f32[512,512]{1,0:T(8,128)} async-done(((f32[16,512]{1,0:T(8,128)}), f32[512,512]{1,0:T(8,128)}) %all-gather.4.cloned.1.call-update) | async-done | bytes 1048592 | tf_op jit(solution)/shard_map/all_gather | solution.py:66
  348.2 1.2 abs_reduce_fusion.2
  349.4 0.6 reduce_max.36
  350.0 0.6 reduce_max.37
  351.9 1.1 fusion.46
  353.2 1.6 fusion.42
  354.9 0.4 convolution_subtract_fusion.16
  361.4 0.7 abs_reduce_fusion
  362.0 0.6 reduce_max.38
  362.6 0.7 reduce_max.39
  363.3 0.6 copy.28
  365.3 0.4 fusion.23
  365.7 0.4 convolution_subtract_fusion.7
  366.1 0.4 fusion.47
  366.9 0.4 fusion.48
  367.8 0.4 fusion.49
  368.6 0.4 fusion.50
  369.4 0.4 fusion.51
  370.2 0.4 fusion.52
  371.0 0.4 fusion.53
  372.3 0.6 copy.29
  (44 shorter events, 9.7 us)
Async XLA Ops:
  7.2 66.9 %all-gather.6.cloned.1.call-start = ((), (), s32[]{:S(2)}) async-start(), calls=%async_computation.2 | async-start | bytes 1671168 | tf_op jit(solution)/shard_map/all_gather | solution.py:42
  7.9 194.0 %reduce-scatter.4.cloned.1.call-start = ((), (), s32[]{:S(2)}) async-start(), calls=%async_computation.3 | async-start | bytes 3244032 | tf_op jit(solution)/shard_map/reduce_scatter | solution.py:64
  8.0 4.7 %copy-start.2 = (s32[512]{0:T(512)S(1)}, s32[512]{0:T(512)}, u32[]{:S(2)}) copy-start(s32[512]{0:T(512)} %param.7) | copy-start | bytes 6148
  8.0 4.7 %copy-start.3 = (f32[32,1]{0,1:T(1,128)S(1)}, f32[32,1]{0,1:T(1,128)}, u32[]{:S(2)}) copy-start(f32[32,1]{0,1:T(1,128)} %param.6) | copy-start | bytes 388
  74.1 5.6 %copy-start.1 = (bf16[1,1536,1024]{2,1,0:T(8,128)(2,1)S(1)}, bf16[1,1536,1024]{2,1,0:T(8,128)(2,1)}, u32[]{:S(2)}) copy-start(bf16[1,1536,1024]{2,1,0:T(8,128)(2,1)} %param.4) | copy-start | bytes 9437188
  90.6 257.6 %all-gather.4.cloned.1.call-start = ((), (), s32[]{:S(2)}) async-start(), calls=%async_computation.1 | async-start | bytes 1081344 | tf_op jit(solution)/shard_map/all_gather | solution.py:66
  348.2 6.7 %copy-start = (f32[512,512]{1,0:T(8,128)S(1)}, f32[512,512]{1,0:T(8,128)}, u32[]{:S(2)}) copy-start(f32[512,512]{1,0:T(8,128)} %all-gather.4.cloned.1.call-done) | copy-start | bytes 3145732
Sparse Core Ops, SparseCore 0:
  11.0 62.9 all-gather.5
  90.8 111.1 reduce-scatter.3
  266.6 81.6 all-gather.3

commit v2 on v1

--- a/solution.py
+++ b/solution.py
@@ -1,10 +1,285 @@
 import jax
 import jax.numpy as jnp
 from jax import lax
+from jax.experimental import pallas as pl
+from jax.experimental.pallas import tpu as pltpu
 from jax.sharding import PartitionSpec as P
 
 HALF = 256
 NEWTON = 8
+GRID = 4
+MESH = pl.DeviceIdType.MESH
+VMEM = pl.BlockSpec(memory_space=pltpu.VMEM)
+
+
+def greet(devices):
+    barrier = pltpu.get_barrier_semaphore()
+    for device in devices:
+        pl.semaphore_signal(barrier, inc=1, device_id=device, device_id_type=MESH)
+    pl.semaphore_wait(barrier, len(devices))
+
+
+def gather_kernel(own_ref, out_ref, send_sem, recv_sem):
+    me = lax.axis_index("row")
+    x, y = me // GRID, me % GRID
+    depth, width = own_ref.shape
+    middle = depth // 2
+    halves = ((0, width // 2), (width // 2, width // 2))
+
+    def index(half, along, across):
+        dx, dy = (across, along) if half == 0 else (along, across)
+        return ((x + dx + GRID) % GRID) * GRID + (y + dy + GRID) % GRID
+
+    greet([{"row": index(0, a, b)} for a, b in ((1, 0), (-1, 0), (0, 1), (0, -1))])
+    out_ref[me] = own_ref[...]
+    sent = []
+
+    def view(half, owner, part):
+        start, size = ((0, depth), (0, middle), (middle, depth - middle))[part]
+        return out_ref.at[owner, pl.ds(start, size), pl.ds(*halves[half])]
+
+    def copy(half, ring, kind, owner, own, target):
+        part = (0, 0, 1, 2)[kind]
+        slot = (half * 5 + ring) * 4 + kind
+        there = view(half, owner, part)
+        source = own_ref.at[:, pl.ds(*halves[half])] if own else there
+        return pltpu.make_async_remote_copy(
+            src_ref=source,
+            dst_ref=there,
+            send_sem=send_sem.at[slot],
+            recv_sem=recv_sem.at[slot],
+            device_id={"row": target},
+            device_id_type=MESH,
+        )
+
+    def place(half, ring, q, step):
+        return index(half, step, 0) if ring == 0 else index(half, q, step)
+
+    def peer(half, ring, step):
+        return index(half, step, 0) if ring == 0 else index(half, 0, step)
+
+    def start(half, ring, q):
+        for kind, step in ((0, 1), (1, -1)):
+            one = copy(half, ring, kind, place(half, ring, q, 0), q == 0, peer(half, ring, step))
+            one.start()
+            sent.append(one)
+
+    def relay(half, ring, q):
+        for kind, step in ((0, 1), (1, -1)):
+            copy(half, ring, kind, place(half, ring, q, -step), False, peer(half, ring, step)).wait_recv()
+            one = copy(half, ring, kind + 2, place(half, ring, q, -step), False, peer(half, ring, step))
+            one.start()
+            sent.append(one)
+
+    def finish(half, ring, q):
+        for kind, step in ((2, 1), (3, -1)):
+            copy(half, ring, kind, place(half, ring, q, 2), False, peer(half, ring, step)).wait_recv()
+
+    order = ((1, 0), (2, -1), (3, 1), (4, 2))
+    for half in range(2):
+        start(half, 0, 0)
+    for half in range(2):
+        start(half, 1, 0)
+    for half in range(2):
+        relay(half, 0, 0)
+        start(half, 2, -1)
+        start(half, 3, 1)
+    for half in range(2):
+        relay(half, 1, 0)
+    for half in range(2):
+        finish(half, 0, 0)
+        start(half, 4, 2)
+    for ring, q in order[1:]:
+        for half in range(2):
+            relay(half, ring, q)
+    for ring, q in order:
+        for half in range(2):
+            finish(half, ring, q)
+    for one in sent:
+        one.wait_send()
+
+
+def gather_solves(own):
+    depth, width = own.shape
+    devices = GRID * GRID
+    return pl.pallas_call(
+        gather_kernel,
+        out_shape=jax.ShapeDtypeStruct((devices, depth, width), own.dtype),
+        in_specs=[VMEM],
+        out_specs=VMEM,
+        scratch_shapes=[pltpu.SemaphoreType.DMA((40,)), pltpu.SemaphoreType.DMA((40,))],
+        compiler_params=pltpu.CompilerParams(collective_id=0, has_side_effects=True),
+        name="gather_solves",
+    )(own).reshape(devices * depth, width)
+
+
+def reduce_kernel(
+    main_ref, extra_ref, diag_ref, both_ref, pivot_ref,
+    got_main, got_extra, acc_main, acc_extra,
+    main_back, main_on, extra_back, extra_on, y_slots, x_slots, stage,
+    send_sem, recv_sem,
+):
+    chips = main_ref.shape[0]
+    far = chips // 2
+    scen = lax.axis_index("scen")
+    me = lax.axis_index("row")
+    z, core = scen // 2, scen % 2
+    x, y = me // GRID, me % GRID
+    partner = {"scen": z * 2 + 1 - core}
+    back = {"scen": ((z + chips - 1) % chips) * 2 + core}
+    on = {"scen": ((z + 1) % chips) * 2 + core}
+    y_peers = [{"row": x * GRID + (y + j) % GRID} for j in range(1, GRID)]
+    x_peers = [{"row": ((x + j) % GRID) * GRID + y} for j in range(1, GRID)]
+    greet([partner, back, on] + y_peers + x_peers)
+    sent = []
+    slots = iter(range(send_sem.shape[0]))
+
+    def copy(source, there, slot, device):
+        return pltpu.make_async_remote_copy(
+            src_ref=source,
+            dst_ref=there,
+            send_sem=send_sem.at[slot],
+            recv_sem=recv_sem.at[slot],
+            device_id=device,
+            device_id_type=MESH,
+        )
+
+    def send(source, there, slot, device):
+        one = copy(source, there, slot, device)
+        one.start()
+        sent.append(one)
+        return one
+
+    swap_extra = send(extra_ref.at[:, 1 - core], got_extra, next(slots), partner)
+    swap_main = send(main_ref.at[:, 1 - core], got_main, next(slots), partner)
+
+    def ring(acc, back_slots, on_slots):
+        back_ids = [next(slots) for _ in range(far)]
+        on_ids = [next(slots) for _ in range(far - 1)]
+        back_sent, on_sent = [], []
+
+        def step(k):
+            if k <= far:
+                to = (z + far + k) % chips
+                if k >= 1:
+                    back_sent[k - 1].wait_recv()
+                    acc[to] = acc[to] + back_slots[k - 1]
+                if k < far:
+                    back_sent.append(send(acc.at[to], back_slots.at[k], back_ids[k], back))
+            if k <= far - 1:
+                to = (z + far - 1 - k) % chips
+                if k >= 1:
+                    on_sent[k - 1].wait_recv()
+                    acc[to] = acc[to] + on_slots[k - 1]
+                if k < far - 1:
+                    on_sent.append(send(acc.at[to], on_slots.at[k], on_ids[k], on))
+
+        return step
+
+    swap_extra.wait_recv()
+    acc_extra[...] = extra_ref[:, core] + got_extra[...]
+    extra_step = ring(acc_extra, extra_back, extra_on)
+    main_step = ring(acc_main, main_back, main_on)
+    extra_step(0)
+    swap_main.wait_recv()
+    acc_main[...] = main_ref[:, core] + got_main[...]
+    for k in range(1, far + 1):
+        extra_step(k)
+    y_sent = [
+        send(acc_extra.at[z], y_slots.at[j], next(slots), device) for j, device in enumerate(y_peers)
+    ]
+    main_step(0)
+    for one in y_sent:
+        one.wait_recv()
+    stage[...] = (acc_extra[z] + y_slots[0]) + (y_slots[1] + y_slots[2])
+    x_sent = [
+        send(stage, x_slots.at[j], next(slots), device) for j, device in enumerate(x_peers)
+    ]
+    main_step(1)
+    for one in x_sent:
+        one.wait_recv()
+    pivot_ref[z, core] = (stage[...] + x_slots[0]) + (x_slots[1] + x_slots[2])
+
+    back_ids = [next(slots) for _ in range(far)]
+    on_ids = [next(slots) for _ in range(far - 1)]
+    share_ids = [next(slots) for _ in range(chips)]
+
+    def block(offset, side):
+        return pivot_ref.at[(z + offset + chips) % chips, side]
+
+    def pass_back(k, offset):
+        return copy(block(offset, core), block(offset, core), back_ids[k], back)
+
+    def pass_on(k, offset):
+        return copy(block(offset, core), block(offset, core), on_ids[k], on)
+
+    def share(offset):
+        send(block(offset, core), block(offset, core), share_ids[offset + far - 1], partner)
+
+    def launch(one):
+        one.start()
+        sent.append(one)
+
+    launch(pass_back(0, 0))
+    launch(pass_on(0, 0))
+    share(0)
+    main_step(2)
+    for k in range(1, far + 1):
+        pass_back(k - 1, k).wait_recv()
+        if k < far:
+            launch(pass_back(k, k))
+        if k < far:
+            pass_on(k - 1, -k).wait_recv()
+            if k < far - 1:
+                launch(pass_on(k, -k))
+            share(-k)
+        share(k)
+        if k + 2 <= far:
+            main_step(k + 2)
+    both_ref[...] = acc_main[z] + diag_ref[...]
+    for offset in range(1 - far, far + 1):
+        copy(
+            block(offset, 1 - core), block(offset, 1 - core), share_ids[offset + far - 1], partner
+        ).wait_recv()
+    for one in sent:
+        one.wait_send()
+
+
+def reduce_and_share(main, extra, diag):
+    rows, panel = main.shape
+    scens = lax.axis_size("scen")
+    chips = scens // 2
+    far = chips // 2
+    share, pivots = rows // scens, panel // scens
+    f32 = jnp.float32
+    count = 2 + 3 * (2 * far - 1) + 2 * (GRID - 1) + chips
+    both, pivot = pl.pallas_call(
+        reduce_kernel,
+        out_shape=(
+            jax.ShapeDtypeStruct((share, panel), f32),
+            jax.ShapeDtypeStruct((chips, 2, pivots, panel), f32),
+        ),
+        in_specs=[VMEM] * 3,
+        out_specs=(VMEM, VMEM),
+        scratch_shapes=[
+            pltpu.VMEM((chips, share, panel), f32),
+            pltpu.VMEM((chips, pivots, panel), f32),
+            pltpu.VMEM((chips, share, panel), f32),
+            pltpu.VMEM((chips, pivots, panel), f32),
+            pltpu.VMEM((far, share, panel), f32),
+            pltpu.VMEM((far - 1, share, panel), f32),
+            pltpu.VMEM((far, pivots, panel), f32),
+            pltpu.VMEM((far - 1, pivots, panel), f32),
+            pltpu.VMEM((GRID - 1, pivots, panel), f32),
+            pltpu.VMEM((GRID - 1, pivots, panel), f32),
+            pltpu.VMEM((pivots, panel), f32),
+            pltpu.SemaphoreType.DMA((count,)),
+            pltpu.SemaphoreType.DMA((count,)),
+        ],
+        compiler_params=pltpu.CompilerParams(collective_id=1, has_side_effects=True),
+        name="reduce_and_share",
+    )(main.reshape(chips, 2, share, panel), extra.reshape(chips, 2, pivots, panel), diag)
+    return both, pivot.reshape(panel, panel)
 
 
 def newton_start(pivot):
@@ -39,11 +314,10 @@
 
 def shards(coupling, solves, border_diagonal, panel_rows):
     scens = lax.axis_size("scen")
-    full_solves = lax.all_gather(solves[0], "row", axis=0, tiled=True)
+    full_solves = gather_solves(solves[0])
     row_count = coupling.shape[2]
     panel = panel_rows.shape[0]
     share = row_count // scens
-    pivot_share = panel // scens
     first_row = lax.axis_index("row") * row_count
     base = first_row + lax.axis_index("scen") * share
     local = first_row + jnp.arange(row_count, dtype=jnp.int32)
@@ -58,12 +332,7 @@
     diag_row = jnp.sum(diag_part, axis=0)
     order = jnp.arange(panel, dtype=jnp.int32)
     extra = extra + jnp.where(order[:, None] == order[None, :], diag_row[:, None], jnp.float32(0.0))
-    joined = jnp.concatenate(
-        [main.reshape(scens, share, panel), extra.reshape(scens, pivot_share, panel)], axis=1
-    ).reshape(scens * (share + pivot_share), panel)
-    summed = lax.psum_scatter(joined, "scen", scatter_dimension=0, tiled=True)
-    both = summed[:share] + diag_part
-    pivots = lax.all_gather(lax.psum(summed[share:], "row"), "scen", axis=0, tiled=True)
+    both, pivots = reduce_and_share(main, extra, diag_part)
     return eliminate(both, pivots)
 
 

time: 380 us -> 143 us (0.38)
  waiting for transfers between devices: 254 us -> 0 us
  Pallas kernels: 0 us -> 98.9 us
  blocking collectives: 62.9 us -> 0 us
  between operations: 16.8 us -> 3.66 us
  other arithmetic: 9.84 us -> 5.43 us
    all_gather x2 -> x0, waiting for transfers between devices: 142 us -> none  [the longest x1 80.9 us: shards(): lax.all_gather(lax.psum(summed[share:], 'row'), 'scen', axis=0, tiled=True)]
    reduce_scatter x1 -> x0, waiting for transfers between devices: 111 us -> none  [shards(): summed = lax.psum_scatter(joined, 'scen', scatter_dimension=0, tiled=True)]
    pallas_call x0 -> x2, Pallas kernels: none -> 98.9 us  [the longest x1 79.4 us: reduce_and_share(): pl.pallas_call(reduce_kernel, out_shape=(jax.ShapeDtypeStruct((share, pan...]
    psum x1 -> x0, blocking collectives: 62.9 us -> none  [shards(): lax.psum(summed[share:], 'row')]
    concatenate x1 -> x0, other arithmetic: 4.1 us -> none  [shards(): jnp.concatenate([main.reshape(scens, share, panel), extra.reshape(scens,...]
  transfers between devices with their start and end apart: 3 -> 0, of which waited for: 3 -> 0; matrix products, arithmetic and copies ran while one was open for 1% -> 0% of each run, Pallas kernels for 0% -> 0%
where the time goes in v2:
time: 143 us; the launch traced here: 142 us
  Pallas kernels  98.9 us (69%)
  matrix products  28.1 us (20%)
  local copies, waits for them, and re-layouts  6.23 us (4%)
  other arithmetic  5.43 us (4%)
  between operations  3.66 us (3%)
    pallas_call x1, Pallas kernels, reduce_and_share(): pl.pallas_call(reduce_kernel, out_shape=(jax.ShapeDtypeStruct((share, pan...  79.4 us
    pallas_call x1, Pallas kernels, gather_solves(): pl.pallas_call(gather_kernel, out_shape=jax.ShapeDtypeStruct((devices, de...  19.4 us
    dot_general x16, matrix products, invert(): left = jnp.dot(approx, pivot, precision=lax.Precision.HIGHEST)  7.61 us
    dot_general x1, matrix products, shards(): jnp.einsum('nr,nc->rc', chosen, full_solves, preferred_element_type=jnp.f...  6.79 us
    dot_general x16, matrix products, invert(): jnp.dot(left, approx, precision=lax.Precision.HIGHEST)  6.31 us
    unnamed x14, local copies, waits for them, and re-layouts  6.1 us
    dot_general x1, matrix products, shards(): jnp.einsum('nr,nc->rc', coupling[0], full_solves, preferred_element_type=...  5.66 us

profile of v2, /device:TPU:1, one launch (start us, length us, event | category | flops | bytes accessed | tf_op | source)
XLA Modules:
  0.0 142.3 jit_solution(3066541482586678277)
XLA Ops:
  0.6 4.6 %copy.13 = bf16[1,1536,1024]{1,2,0:T(8,128)(2,1)} copy(bf16[1,1536,1024]{2,1,0:T(8,128)(2,1)} %param.4) | data formatting | bytes 6291456 | tf_op args[0]
  5.3 19.4 %gather_solves.1 = bf16[16,96,512]{2,1,0:T(8,128)(2,1)} custom-call(bf16[96,512]{1,0:T(8,128)(2,1)} %bitcast.108), custom_call_target="tpu_custom_call" | custom-call | tf_op jit(solution)/shard_map/gather_solves/pallas_call | solution.py:105
  24.7 5.7 %fusion.41.main_ref = f32[16,2,32,512]{3,2,1,0:T(8,128)} fusion(bf16[16,2,32,1536]{3,2,1,0:T(8,128)(2,1)} %bitcast.103, bf16[1536,512,1,1]{1,0,3,2:T(8,128)(2,1)} %bitcast.104), kind=kOutput, calls=%fused_computation.65 | convolution fusion | flops 1610612736 | bytes 6815744 | tf_op jit(solution)/shard_map/nr,nc->rc/dot_general | solution.py:330
  30.4 0.7 compare_select_fusion
  31.1 6.8 %convolution_add_fusion = f32[512,512]{1,0:T(8,128)} fusion(bf16[1536,512]{1,0:T(8,128)(2,1)} %bitcast.105, bf16[1,1536,1024]{2,1,0:T(8,128)(2,1)S(1)} %copy-done.1, s32[512]{0:T(512)S(1)} %copy-done.3, s32[1024]{0:T(1024)S(1)} %iota_add_fusion, f32[512]{0:T(512)S(1)} %get-tuple-element.17), kind=kOutput, calls=%fused_computation.4 | convolution fusion | flops 2418016256 | bytes 5775360 | tf_op jit(solution)/shard_map/nr,nc->rc/dot_general | solution.py:331
  37.9 79.4 %reduce_and_share.1 = (f32[32,512]{1,0:T(8,128)}, f32[16,2,16,512]{3,2,1,0:T(8,128)}) custom-call(f32[16,2,32,512]{3,2,1,0:T(8,128)} %fusion.41.main_ref, f32[16,2,16,512]{3,2,1,0:T(8,128)} %bitcast.106, f32[32,512]{1,0:T(8,128)} %get-tuple-element.16.diag_ref), custom_call_target="tpu_custom_call" | custom-call | tf_op jit(solution)/shard_map/reduce_and_share/pallas_call | solution.py:256
  117.4 1.2 abs_reduce_fusion.2
  118.5 0.6 reduce_max.36
  119.1 0.6 reduce_max.37
  121.0 1.1 fusion.40
  122.2 1.7 %fusion.35 = f32[256,256]{1,0:T(8,128)S(1)} fusion(f32[512,512]{1,0:T(8,128)} %bitcast.91, f32[]{:T(128)S(6)} %mul.68), kind=kOutput, calls=%fused_computation.56 | convolution fusion | flops 201392128 | bytes 786436 | tf_op jit(solution)/shard_map/dot_general | solution.py:294
  123.9 0.4 convolution_subtract_fusion.16
  126.3 0.4 convolution_subtract_fusion.13
  128.6 0.6 convolution_subtract_fusion.10
  130.2 0.6 copy.18
  131.6 0.7 abs_reduce_fusion
  132.3 0.6 reduce_max.38
  132.9 0.7 reduce_max.39
  135.0 0.4 fusion.16
  135.4 0.4 convolution_subtract_fusion.7
  135.8 0.4 fusion.42
  136.2 0.4 convolution_subtract_fusion.6
  136.6 0.4 fusion.43
  137.4 0.4 fusion.44
  137.8 0.4 convolution_subtract_fusion.4
  138.2 0.4 fusion.45
  138.6 0.4 convolution_subtract_fusion.3
  139.0 0.4 fusion.46
  139.8 0.4 fusion.47
  140.2 0.4 convolution_subtract_fusion.1
  140.6 0.4 fusion.48
  141.7 0.6 copy.19
  (33 shorter events, 7.1 us)
Async XLA Ops:
  24.7 5.7 %copy-start.3 = (s32[512]{0:T(512)S(1)}, s32[512]{0:T(512)}, u32[]{:S(2)}) copy-start(s32[512]{0:T(512)} %param.7) | copy-start | bytes 6148
  24.7 5.7 %copy-start.4 = (f32[32,1]{0,1:T(1,128)S(1)}, f32[32,1]{0,1:T(1,128)}, u32[]{:S(2)}) copy-start(f32[32,1]{0,1:T(1,128)} %param.6) | copy-start | bytes 388
  24.7 6.4 %copy-start.1 = (bf16[1,1536,1024]{2,1,0:T(8,128)(2,1)S(1)}, bf16[1,1536,1024]{2,1,0:T(8,128)(2,1)}, u32[]{:S(2)}) copy-start(bf16[1,1536,1024]{2,1,0:T(8,128)(2,1)} %param.4) | copy-start | bytes 9437188
  117.4 6.6 %copy-start = (f32[16,2,16,512]{3,2,1,0:T(8,128)S(1)}, f32[16,2,16,512]{3,2,1,0:T(8,128)}, u32[]{:S(2)}) copy-start(f32[16,2,16,512]{3,2,1,0:T(8,128)} %get-tuple-element.5) | copy-start | bytes 3145732
  127.9 2.1 %copy-start.2 = (f32[32,512]{1,0:T(8,128)S(1)}, f32[32,512]{1,0:T(8,128)}, u32[]{:S(2)}) copy-start(f32[32,512]{1,0:T(8,128)} %get-tuple-element.4) | copy-start | bytes 196612

commit v3 on v2

--- a/solution.py
+++ b/solution.py
@@ -282,34 +282,63 @@
     return both, pivot.reshape(panel, panel)
 
 
-def newton_start(pivot):
-    norm_one = jnp.max(jnp.sum(jnp.abs(pivot), axis=0))
-    norm_inf = jnp.max(jnp.sum(jnp.abs(pivot), axis=1))
-    return pivot.T / (norm_one * norm_inf)
-
-
-def invert(pivot):
-    approx = newton_start(pivot)
-    for step in range(NEWTON):
-        left = jnp.dot(approx, pivot, precision=lax.Precision.HIGHEST)
-        approx = 2.0 * approx - jnp.dot(left, approx, precision=lax.Precision.HIGHEST)
-    return approx
+def exact(a, b):
+    return jnp.dot(a, b, precision=lax.Precision.HIGHEST, preferred_element_type=jnp.float32)
+
+
+def split(a):
+    high = a.astype(jnp.bfloat16)
+    return high, (a - high.astype(jnp.float32)).astype(jnp.bfloat16)
+
+
+def split_dot(a, b):
+    def dot(p, q):
+        return jnp.dot(p, q, preferred_element_type=jnp.float32)
+
+    return dot(a[0], b[0]) + (dot(a[0], b[1]) + dot(a[1], b[0]))
+
+
+def invert(pivot, approx_ref):
+    size = jnp.abs(pivot)
+    norm_one = jnp.max(jnp.sum(size, axis=0, keepdims=True), axis=1, keepdims=True)
+    norm_inf = jnp.max(jnp.sum(size, axis=1, keepdims=True), axis=0, keepdims=True)
+    approx_ref[...] = pivot.T / (norm_one * norm_inf)
+    parts = split(pivot)
+
+    def step(_, carry):
+        approx = approx_ref[...]
+        both = split(approx)
+        left = split(split_dot(both, parts))
+        approx_ref[...] = 2.0 * approx - split_dot(left, both)
+        return carry
+
+    lax.fori_loop(0, NEWTON - 1, step, 0)
+    approx = approx_ref[...]
+    return 2.0 * approx - exact(exact(approx, pivot), approx)
+
+
+def eliminate_kernel(both_ref, pivot_ref, first_ref, second_ref, approx_ref):
+    inverse_first = invert(pivot_ref[:HALF, :HALF], approx_ref)
+    upper = pivot_ref[:HALF, HALF:]
+    first = exact(both_ref[:, :HALF], inverse_first)
+    first_ref[...] = first
+    lower = exact(pivot_ref[HALF:, :HALF], inverse_first)
+    pivot_two = pivot_ref[HALF:, HALF:] - exact(lower, upper)
+    updated = both_ref[:, HALF:] - exact(first, upper)
+    second_ref[...] = exact(updated, invert(pivot_two, approx_ref))
 
 
 def eliminate(both, pivots):
-    first = both[:, :HALF]
-    second = both[:, HALF:]
-    inverse_first = invert(pivots[:HALF, :HALF])
-    first_factor = jnp.dot(first, inverse_first, precision=lax.Precision.HIGHEST)
-    upper = pivots[:HALF, HALF:]
-    updated = second - jnp.dot(first_factor, upper, precision=lax.Precision.HIGHEST)
-    lower_factor = jnp.dot(pivots[HALF:, :HALF], inverse_first, precision=lax.Precision.HIGHEST)
-    pivot_two = pivots[HALF:, HALF:] - jnp.dot(
-        lower_factor, upper, precision=lax.Precision.HIGHEST
-    )
-    inverse_second = invert(pivot_two)
-    second_factor = jnp.dot(updated, inverse_second, precision=lax.Precision.HIGHEST)
-    return (first_factor[:, None, :], second_factor[:, None, :])
+    half = jax.ShapeDtypeStruct((both.shape[0], HALF), jnp.float32)
+    first, second = pl.pallas_call(
+        eliminate_kernel,
+        out_shape=(half, half),
+        in_specs=[VMEM, VMEM],
+        out_specs=(VMEM, VMEM),
+        scratch_shapes=[pltpu.VMEM((HALF, HALF), jnp.float32)],
+        name="eliminate",
+    )(both, pivots)
+    return first[:, None, :], second[:, None, :]
 
 
 def shards(coupling, solves, border_diagonal, panel_rows):

time: 143 us -> 135 us (0.944)
  matrix products: 28.1 us -> 12.4 us
  Pallas kernels: 98.9 us -> 113 us
  other arithmetic: 5.43 us -> 0.7 us
  between operations: 3.66 us -> 0.68 us
    dot_general x37 -> x0, matrix products: 15.7 us -> none  [the longest x16 7.61 us: invert(): left = jnp.dot(approx, pivot, precision=lax.Precision.HIGHEST)]
    pallas_call x0 -> x1, Pallas kernels: none -> 14 us  [eliminate(): pl.pallas_call(eliminate_kernel, out_shape=(half, half), in_specs=[VMEM,...]
    reduce_max x4 -> x0, other arithmetic: 2.49 us -> none  [the longest x2 1.28 us: newton_start(): norm_inf = jnp.max(jnp.sum(jnp.abs(pivot), axis=1))]
    unnamed x14 -> x9, local copies, waits for them, and re-layouts: 6.1 us -> 7.49 us
where the time goes in v3:
time: 135 us; the launch traced here: 134 us
  Pallas kernels  113 us (84%)
  matrix products  12.4 us (9%)
  local copies, waits for them, and re-layouts  7.49 us (6%)
    pallas_call x1, Pallas kernels, reduce_and_share(): pl.pallas_call(reduce_kernel, out_shape=(jax.ShapeDtypeStruct((share, pan...  79.4 us
    pallas_call x1, Pallas kernels, gather_solves(): pl.pallas_call(gather_kernel, out_shape=jax.ShapeDtypeStruct((devices, de...  19.4 us
    pallas_call x1, Pallas kernels, eliminate(): pl.pallas_call(eliminate_kernel, out_shape=(half, half), in_specs=[VMEM,...  14 us
    unnamed x9, local copies, waits for them, and re-layouts  7.49 us
    dot_general x1, matrix products, shards(): jnp.einsum('nr,nc->rc', chosen, full_solves, preferred_element_type=jnp.f...  6.77 us
    dot_general x1, matrix products, shards(): jnp.einsum('nr,nc->rc', coupling[0], full_solves, preferred_element_type=...  5.64 us

profile of v3, /device:TPU:1, one launch (start us, length us, event | category | flops | bytes accessed | tf_op | source)
XLA Modules:
  0.0 134.1 jit_solution(9246983807592294487)
XLA Ops:
  0.6 4.7 %copy.9 = bf16[1,1536,1024]{1,2,0:T(8,128)(2,1)} copy(bf16[1,1536,1024]{2,1,0:T(8,128)(2,1)} %param.4) | data formatting | bytes 6291456 | tf_op args[0]
  5.3 19.4 %gather_solves.1 = bf16[16,96,512]{2,1,0:T(8,128)(2,1)} custom-call(bf16[96,512]{1,0:T(8,128)(2,1)} %bitcast.31), custom_call_target="tpu_custom_call" | custom-call | tf_op jit(solution)/shard_map/gather_solves/pallas_call | solution.py:105
  24.7 0.0 copy-start.1
  24.7 0.0 copy-start.2
  24.7 0.0 copy-start
  24.7 5.6 %fusion.13.main_ref = f32[16,2,32,512]{3,2,1,0:T(8,128)} fusion(bf16[16,2,32,1536]{3,2,1,0:T(8,128)(2,1)} %bitcast.26, bf16[1536,512,1,1]{1,0,3,2:T(8,128)(2,1)} %bitcast.27), kind=kOutput, calls=%fused_computation.12 | convolution fusion | flops 1610612736 | bytes 6815744 | tf_op jit(solution)/shard_map/nr,nc->rc/dot_general | solution.py:359
  30.4 0.0 copy-done.1
  30.4 0.0 copy-done.2
  30.4 0.7 compare_select_fusion
  31.1 0.0 copy-done
  31.1 6.8 %convolution_add_fusion = f32[512,512]{1,0:T(8,128)} fusion(bf16[1536,512]{1,0:T(8,128)(2,1)} %bitcast.28, bf16[1,1536,1024]{2,1,0:T(8,128)(2,1)S(1)} %copy-done, s32[512]{0:T(512)S(1)} %copy-done.1, s32[1024]{0:T(1024)S(1)} %iota_add_fusion, f32[512]{0:T(512)S(1)} %get-tuple-element.15), kind=kOutput, calls=%fused_computation.4 | convolution fusion | flops 2418016256 | bytes 5775360 | tf_op jit(solution)/shard_map/nr,nc->rc/dot_general | solution.py:360
  37.9 79.4 %reduce_and_share.1 = (f32[32,512]{1,0:T(8,128)}, f32[16,2,16,512]{3,2,1,0:T(8,128)}) custom-call(f32[16,2,32,512]{3,2,1,0:T(8,128)} %fusion.13.main_ref, f32[16,2,16,512]{3,2,1,0:T(8,128)} %bitcast.29, f32[32,512]{1,0:T(8,128)} %get-tuple-element.14.diag_ref), custom_call_target="tpu_custom_call" | custom-call | tf_op jit(solution)/shard_map/reduce_and_share/pallas_call | solution.py:256
  117.3 14.0 %eliminate.1 = (f32[32,256]{1,0:T(8,128)}, f32[32,256]{1,0:T(8,128)}) custom-call(f32[32,512]{1,0:T(8,128)} %get-tuple-element.6.both_ref, f32[512,512]{1,0:T(8,128)} %bitcast.30), custom_call_target="tpu_custom_call" | custom-call | tf_op jit(solution)/shard_map/eliminate/pallas_call | solution.py:333
  131.3 1.4 %copy.10 = f32[32,1,256]{2,1,0:T(1,128)} copy(f32[32,1,256]{2,0,1:T(8,128)} %bitcast.33) | data formatting | bytes 65536
  132.7 1.4 %copy.11 = f32[32,1,256]{2,1,0:T(1,128)} copy(f32[32,1,256]{2,0,1:T(8,128)} %bitcast.32) | data formatting | bytes 65536
  (2 shorter events, 0.0 us)
Async XLA Ops:
  24.7 5.7 %copy-start.1 = (s32[512]{0:T(512)S(1)}, s32[512]{0:T(512)}, u32[]{:S(2)}) copy-start(s32[512]{0:T(512)} %param.7) | copy-start | bytes 6148
  24.7 5.7 %copy-start.2 = (f32[32,1]{0,1:T(1,128)S(1)}, f32[32,1]{0,1:T(1,128)}, u32[]{:S(2)}) copy-start(f32[32,1]{0,1:T(1,128)} %param.6) | copy-start | bytes 388
  24.7 6.4 %copy-start = (bf16[1,1536,1024]{2,1,0:T(8,128)(2,1)S(1)}, bf16[1,1536,1024]{2,1,0:T(8,128)(2,1)}, u32[]{:S(2)}) copy-start(bf16[1,1536,1024]{2,1,0:T(8,128)(2,1)} %param.4) | copy-start | bytes 9437188

commit v4 on v3

--- a/solution.py
+++ b/solution.py
@@ -8,6 +8,7 @@
 HALF = 256
 NEWTON = 8
 GRID = 4
+MIB = 1 << 20
 MESH = pl.DeviceIdType.MESH
 VMEM = pl.BlockSpec(memory_space=pltpu.VMEM)
 
@@ -108,7 +109,9 @@
         in_specs=[VMEM],
         out_specs=VMEM,
         scratch_shapes=[pltpu.SemaphoreType.DMA((40,)), pltpu.SemaphoreType.DMA((40,))],
-        compiler_params=pltpu.CompilerParams(collective_id=0, has_side_effects=True),
+        compiler_params=pltpu.CompilerParams(
+            collective_id=0, has_side_effects=True, vmem_limit_bytes=8 * MIB
+        ),
         name="gather_solves",
     )(own).reshape(devices * depth, width)
 
@@ -276,7 +279,9 @@
             pltpu.SemaphoreType.DMA((count,)),
             pltpu.SemaphoreType.DMA((count,)),
         ],
-        compiler_params=pltpu.CompilerParams(collective_id=1, has_side_effects=True),
+        compiler_params=pltpu.CompilerParams(
+            collective_id=1, has_side_effects=True, vmem_limit_bytes=16 * MIB
+        ),
         name="reduce_and_share",
     )(main.reshape(chips, 2, share, panel), extra.reshape(chips, 2, pivots, panel), diag)
     return both, pivot.reshape(panel, panel)
@@ -321,24 +326,65 @@
     inverse_first = invert(pivot_ref[:HALF, :HALF], approx_ref)
     upper = pivot_ref[:HALF, HALF:]
     first = exact(both_ref[:, :HALF], inverse_first)
-    first_ref[...] = first
+    first_ref[...] = first[:, None, :]
     lower = exact(pivot_ref[HALF:, :HALF], inverse_first)
     pivot_two = pivot_ref[HALF:, HALF:] - exact(lower, upper)
     updated = both_ref[:, HALF:] - exact(first, upper)
-    second_ref[...] = exact(updated, invert(pivot_two, approx_ref))
+    second_ref[...] = exact(updated, invert(pivot_two, approx_ref))[:, None, :]
 
 
 def eliminate(both, pivots):
-    half = jax.ShapeDtypeStruct((both.shape[0], HALF), jnp.float32)
-    first, second = pl.pallas_call(
+    half = jax.ShapeDtypeStruct((both.shape[0], 1, HALF), jnp.float32)
+    return pl.pallas_call(
         eliminate_kernel,
         out_shape=(half, half),
         in_specs=[VMEM, VMEM],
         out_specs=(VMEM, VMEM),
         scratch_shapes=[pltpu.VMEM((HALF, HALF), jnp.float32)],
+        compiler_params=pltpu.CompilerParams(vmem_limit_bytes=16 * MIB),
         name="eliminate",
     )(both, pivots)
-    return first[:, None, :], second[:, None, :]
+
+
+TILE = 256
+
+
+def product_kernel(coupling_ref, solves_ref, pick_ref, main_ref, extra_ref, chosen_ref):
+    depth, rows = coupling_ref.shape
+    panel = solves_ref.shape[1]
+
+    def dot(a, b):
+        return jnp.dot(a, b, preferred_element_type=jnp.float32)
+
+    def across(a, b):
+        return lax.dot_general(a, b, (((0,), (0,)), ((), ())), preferred_element_type=jnp.float32)
+
+    for at in range(0, depth, TILE):
+        part = pl.ds(at, TILE)
+        chosen_ref[part, :] = dot(coupling_ref[part, :], pick_ref[...]).astype(jnp.bfloat16)
+    for at in range(0, panel, TILE):
+        part = pl.ds(at, TILE)
+        extra_ref[part, :] = across(chosen_ref[:, part], solves_ref[...])
+    for at in range(0, rows, TILE):
+        part = pl.ds(at, TILE)
+        main_ref[part, :] = across(coupling_ref[:, part], solves_ref[...])
+
+
+def products(coupling, full_solves, pick):
+    depth, rows = coupling.shape
+    panel = full_solves.shape[1]
+    return pl.pallas_call(
+        product_kernel,
+        out_shape=(
+            jax.ShapeDtypeStruct((rows, panel), jnp.float32),
+            jax.ShapeDtypeStruct((panel, panel), jnp.float32),
+        ),
+        in_specs=[VMEM] * 3,
+        out_specs=(VMEM, VMEM),
+        scratch_shapes=[pltpu.VMEM((depth, panel), jnp.bfloat16)],
+        compiler_params=pltpu.CompilerParams(vmem_limit_bytes=28 * MIB),
+        name="products",
+    )(coupling, full_solves, pick)
 
 
 def shards(coupling, solves, border_diagonal, panel_rows):
@@ -351,13 +397,11 @@
     base = first_row + lax.axis_index("scen") * share
     local = first_row + jnp.arange(row_count, dtype=jnp.int32)
     pick = (local[:, None] == panel_rows[None, :]).astype(jnp.bfloat16)
-    chosen = jnp.dot(coupling[0], pick, preferred_element_type=jnp.float32).astype(jnp.bfloat16)
     glob = base + jnp.arange(share, dtype=jnp.int32)
     diag_part = jnp.where(
         glob[:, None] == panel_rows[None, :], border_diagonal[:, 0][:, None], jnp.float32(0.0)
     )
-    main = jnp.einsum("nr,nc->rc", coupling[0], full_solves, preferred_element_type=jnp.float32)
-    extra = jnp.einsum("nr,nc->rc", chosen, full_solves, preferred_element_type=jnp.float32)
+    main, extra = products(coupling[0], full_solves, pick)
     diag_row = jnp.sum(diag_part, axis=0)
     order = jnp.arange(panel, dtype=jnp.int32)
     extra = extra + jnp.where(order[:, None] == order[None, :], diag_row[:, None], jnp.float32(0.0))

time: 135 us -> 118 us (0.87)
  matrix products: 12.4 us -> 0 us
  local copies, waits for them, and re-layouts: 7.49 us -> 5.45 us
  Pallas kernels: 113 us -> 111 us
    dot_general x2 -> x0, matrix products: 12.4 us -> none  [the longest x1 6.77 us: shards(): jnp.einsum('nr,nc->rc', chosen, full_solves, preferred_element_type=jnp.f...]
    pallas_call x0 -> x1, Pallas kernels: none -> 4.22 us  [products(): pl.pallas_call(product_kernel, out_shape=(jax.ShapeDtypeStruct((rows, pan...]
    pallas_call x1, Pallas kernels: 79.4 us -> 76.4 us  [reduce_and_share(): pl.pallas_call(reduce_kernel, out_shape=(jax.ShapeDtypeStruct((share, pan...]
    unnamed x9 -> x12, local copies, waits for them, and re-layouts: 7.49 us -> 5.45 us
    pallas_call x1, Pallas kernels: 19.4 us -> 17.4 us  [gather_solves(): pl.pallas_call(gather_kernel, out_shape=jax.ShapeDtypeStruct((devices, de...]
where the time goes in v4:
time: 118 us
  Pallas kernels  111 us (94%)
  local copies, waits for them, and re-layouts  5.45 us (5%)
    pallas_call x1, Pallas kernels, reduce_and_share(): pl.pallas_call(reduce_kernel, out_shape=(jax.ShapeDtypeStruct((share, pan...  76.4 us
    pallas_call x1, Pallas kernels, gather_solves(): pl.pallas_call(gather_kernel, out_shape=jax.ShapeDtypeStruct((devices, de...  17.4 us
    pallas_call x1, Pallas kernels, eliminate(): pl.pallas_call(eliminate_kernel, out_shape=(half, half), in_specs=[VMEM,...  12.8 us
    unnamed x12, local copies, waits for them, and re-layouts  5.45 us
    pallas_call x1, Pallas kernels, products(): pl.pallas_call(product_kernel, out_shape=(jax.ShapeDtypeStruct((rows, pan...  4.22 us

profile of v4, /device:TPU:1, one launch (start us, length us, event | category | flops | bytes accessed | tf_op | source)
XLA Modules:
  0.0 118.2 jit_solution(1793225085930884549)
XLA Ops:
  0.6 0.0 copy-start.3
  0.6 0.9 copy-done.3
  1.5 17.4 %gather_solves.1 = bf16[16,96,512]{2,1,0:T(8,128)(2,1)S(1)} custom-call(bf16[96,512]{1,0:T(8,128)(2,1)S(1)} %bitcast.12), custom_call_target="tpu_custom_call" | custom-call | tf_op jit(solution)/shard_map/gather_solves/pallas_call | solution.py:106
  18.9 0.9 compare_convert_fusion.pick_ref
  19.9 0.0 copy-start
  19.9 1.9 %copy-done = bf16[1,1536,1024]{2,1,0:T(8,128)(2,1)S(1)} copy-done((bf16[1,1536,1024]{2,1,0:T(8,128)(2,1)S(1)}, bf16[1,1536,1024]{2,1,0:T(8,128)(2,1)}, u32[]{:S(2)}) %copy-start) | copy-done | bytes 3145752
  21.7 0.0 copy-start.4
  21.7 0.0 copy-start.5
  21.8 4.2 %products.1 = (f32[1024,512]{1,0:T(8,128)S(1)}, f32[512,512]{1,0:T(8,128)S(1)}) custom-call(bf16[1536,1024]{1,0:T(8,128)(2,1)S(1)} %bitcast.9, bf16[1536,512]{1,0:T(8,128)(2,1)S(1)} %bitcast.7, bf16[1024,512]{1,0:T(8,128)(2,1)S(1)} %compare_convert_fusion.pick_ref), custom_call_target="tpu_custom_call" | custom-call | tf_op jit(solution)/shard_map/products/pallas_call | solution.py:376
  26.0 0.0 copy-start.1
  26.0 1.3 %copy-done.1 = f32[1024,512]{1,0:T(8,128)} copy-done((f32[1024,512]{1,0:T(8,128)}, f32[1024,512]{1,0:T(8,128)S(1)}, u32[]{:S(2)}) %copy-start.1) | copy-done | bytes 2097176
  27.3 0.0 copy-start.2
  27.3 0.0 copy-done.4
  27.3 0.0 copy-done.5
  27.3 0.1 compare_select_fusion
  27.4 0.2 select_add_fusion
  27.6 1.3 %copy-done.2 = f32[1024,512]{1,0:T(8,128)S(1)} copy-done((f32[1024,512]{1,0:T(8,128)S(1)}, f32[1024,512]{1,0:T(8,128)}, u32[]{:S(2)}) %copy-start.2) | copy-done | bytes 2097176
  28.9 76.4 %reduce_and_share.1 = (f32[32,512]{1,0:T(8,128)S(1)}, f32[16,2,16,512]{3,2,1,0:T(8,128)S(1)}) custom-call(f32[16,2,32,512]{3,2,1,0:T(8,128)S(1)} %bitcast.10, f32[16,2,16,512]{3,2,1,0:T(8,128)S(1)} %bitcast.8, f32[32,512]{1,0:T(8,128)S(1)} %get-tuple-element.10.diag_ref), custom_call_target="tpu_custom_call" | custom-call | tf_op jit(solution)/shard_map/reduce_and_share/pallas_call | solution.py:259
  105.4 12.8 %eliminate.1 = (f32[32,1,256]{2,1,0:T(1,128)}, f32[32,1,256]{2,1,0:T(1,128)}) custom-call(f32[32,512]{1,0:T(8,128)S(1)} %get-tuple-element.8.both_ref, f32[512,512]{1,0:T(8,128)S(1)} %bitcast.11), custom_call_target="tpu_custom_call" | custom-call | tf_op jit(solution)/shard_map/eliminate/pallas_call | solution.py:338
  (2 shorter events, 0.0 us)
Async XLA Ops:
  0.6 0.9 copy-start.3
  19.9 1.9 %copy-start = (bf16[1,1536,1024]{2,1,0:T(8,128)(2,1)S(1)}, bf16[1,1536,1024]{2,1,0:T(8,128)(2,1)}, u32[]{:S(2)}) copy-start(bf16[1,1536,1024]{2,1,0:T(8,128)(2,1)} %param.4) | copy-start | bytes 9437188
  21.7 5.6 %copy-start.4 = (s32[512]{0:T(512)S(1)}, s32[512]{0:T(512)}, u32[]{:S(2)}) copy-start(s32[512]{0:T(512)} %param.7) | copy-start | bytes 6148
  21.7 5.6 %copy-start.5 = (f32[32,1]{0,1:T(1,128)S(1)}, f32[32,1]{0,1:T(1,128)}, u32[]{:S(2)}) copy-start(f32[32,1]{0,1:T(1,128)} %param.6) | copy-start | bytes 388
  26.0 1.4 %copy-start.1 = (f32[1024,512]{1,0:T(8,128)}, f32[1024,512]{1,0:T(8,128)S(1)}, u32[]{:S(2)}) copy-start(f32[1024,512]{1,0:T(8,128)S(1)} %get-tuple-element.6) | copy-start | bytes 6291460
  27.3 1.6 %copy-start.2 = (f32[1024,512]{1,0:T(8,128)S(1)}, f32[1024,512]{1,0:T(8,128)}, u32[]{:S(2)}) copy-start(f32[1024,512]{1,0:T(8,128)} %copy-done.1) | copy-start | bytes 6291460

commit v5 on v4

--- a/solution.py
+++ b/solution.py
@@ -186,19 +186,21 @@
     extra_step(0)
     swap_main.wait_recv()
     acc_main[...] = main_ref[:, core] + got_main[...]
-    for k in range(1, far + 1):
+    for k in range(1, far):
         extra_step(k)
+    main_step(0)
+    extra_step(far)
     y_sent = [
         send(acc_extra.at[z], y_slots.at[j], next(slots), device) for j, device in enumerate(y_peers)
     ]
-    main_step(0)
+    main_step(1)
     for one in y_sent:
         one.wait_recv()
     stage[...] = (acc_extra[z] + y_slots[0]) + (y_slots[1] + y_slots[2])
     x_sent = [
         send(stage, x_slots.at[j], next(slots), device) for j, device in enumerate(x_peers)
     ]
-    main_step(1)
+    main_step(2)
     for one in x_sent:
         one.wait_recv()
     pivot_ref[z, core] = (stage[...] + x_slots[0]) + (x_slots[1] + x_slots[2])
@@ -226,7 +228,7 @@
     launch(pass_back(0, 0))
     launch(pass_on(0, 0))
     share(0)
-    main_step(2)
+    main_step(3)
     for k in range(1, far + 1):
         pass_back(k - 1, k).wait_recv()
         if k < far:
@@ -237,8 +239,8 @@
                 launch(pass_on(k, -k))
             share(-k)
         share(k)
-        if k + 2 <= far:
-            main_step(k + 2)
+        if k + 3 <= far:
+            main_step(k + 3)
     both_ref[...] = acc_main[z] + diag_ref[...]
     for offset in range(1 - far, far + 1):
         copy(
@@ -349,7 +351,7 @@
 TILE = 256
 
 
-def product_kernel(coupling_ref, solves_ref, pick_ref, main_ref, extra_ref, chosen_ref):
+def product_kernel(coupling_ref, solves_ref, pick_ref, diag_ref, main_ref, extra_ref, chosen_ref):
     depth, rows = coupling_ref.shape
     panel = solves_ref.shape[1]
 
@@ -364,13 +366,16 @@
         chosen_ref[part, :] = dot(coupling_ref[part, :], pick_ref[...]).astype(jnp.bfloat16)
     for at in range(0, panel, TILE):
         part = pl.ds(at, TILE)
-        extra_ref[part, :] = across(chosen_ref[:, part], solves_ref[...])
+        row = at + lax.broadcasted_iota(jnp.int32, (TILE, panel), 0)
+        column = lax.broadcasted_iota(jnp.int32, (TILE, panel), 1)
+        diag = jnp.where(row == column, diag_ref[part, :], jnp.float32(0.0))
+        extra_ref[part, :] = across(chosen_ref[:, part], solves_ref[...]) + diag
     for at in range(0, rows, TILE):
         part = pl.ds(at, TILE)
         main_ref[part, :] = across(coupling_ref[:, part], solves_ref[...])
 
 
-def products(coupling, full_solves, pick):
+def products(coupling, full_solves, pick, diag):
     depth, rows = coupling.shape
     panel = full_solves.shape[1]
     return pl.pallas_call(
@@ -379,12 +384,12 @@
             jax.ShapeDtypeStruct((rows, panel), jnp.float32),
             jax.ShapeDtypeStruct((panel, panel), jnp.float32),
         ),
-        in_specs=[VMEM] * 3,
+        in_specs=[VMEM] * 4,
         out_specs=(VMEM, VMEM),
         scratch_shapes=[pltpu.VMEM((depth, panel), jnp.bfloat16)],
         compiler_params=pltpu.CompilerParams(vmem_limit_bytes=28 * MIB),
         name="products",
-    )(coupling, full_solves, pick)
+    )(coupling, full_solves, pick, diag)
 
 
 def shards(coupling, solves, border_diagonal, panel_rows):
@@ -401,10 +406,9 @@
     diag_part = jnp.where(
         glob[:, None] == panel_rows[None, :], border_diagonal[:, 0][:, None], jnp.float32(0.0)
     )
-    main, extra = products(coupling[0], full_solves, pick)
-    diag_row = jnp.sum(diag_part, axis=0)
-    order = jnp.arange(panel, dtype=jnp.int32)
-    extra = extra + jnp.where(order[:, None] == order[None, :], diag_row[:, None], jnp.float32(0.0))
+    diag_row = jnp.sum(diag_part, axis=0)[:, None]
+    full_solves, diag_part, diag_row = lax.optimization_barrier((full_solves, diag_part, diag_row))
+    main, extra = products(coupling[0], full_solves, pick, diag_row)
     both, pivots = reduce_and_share(main, extra, diag_part)
     return eliminate(both, pivots)
 

time: 118 us -> 116 us (0.983)
  local copies, waits for them, and re-layouts: 5.45 us -> 2.92 us
    unnamed x12 -> x4, local copies, waits for them, and re-layouts: 5.45 us -> 2.78 us
where the time goes in v5:
time: 116 us
  Pallas kernels  110 us (95%)
  local copies, waits for them, and re-layouts  2.92 us (3%)
  other arithmetic  1.72 us (1%)
    pallas_call x1, Pallas kernels, reduce_and_share(): pl.pallas_call(reduce_kernel, out_shape=(jax.ShapeDtypeStruct((share, pan...  75.8 us
    pallas_call x1, Pallas kernels, gather_solves(): pl.pallas_call(gather_kernel, out_shape=jax.ShapeDtypeStruct((devices, de...  17.4 us
    pallas_call x1, Pallas kernels, eliminate(): pl.pallas_call(eliminate_kernel, out_shape=(half, half), in_specs=[VMEM,...  12.8 us
    pallas_call x1, Pallas kernels, products(): pl.pallas_call(product_kernel, out_shape=(jax.ShapeDtypeStruct((rows, pan...  4.27 us
    unnamed x4, local copies, waits for them, and re-layouts  2.78 us

profile of v5, /device:TPU:1, one launch (start us, length us, event | category | flops | bytes accessed | tf_op | source)
XLA Modules:
  0.0 115.5 jit_solution(14628990315006257535)
XLA Ops:
  0.7 0.8 fusion
  1.5 0.9 compare_convert_fusion.pick_ref
  2.4 0.0 copy-start.1
  2.4 0.9 copy-done.1
  3.3 17.4 %gather_solves.1 = bf16[16,96,512]{2,1,0:T(8,128)(2,1)S(1)} custom-call(bf16[96,512]{1,0:T(8,128)(2,1)S(1)} %bitcast.13), custom_call_target="tpu_custom_call" | custom-call | tf_op jit(solution)/shard_map/gather_solves/pallas_call | solution.py:106
  20.7 0.1 copy.6.diag_ref
  20.8 0.0 copy-start
  20.8 1.9 %copy-done = bf16[1,1536,1024]{2,1,0:T(8,128)(2,1)S(1)} copy-done((bf16[1,1536,1024]{2,1,0:T(8,128)(2,1)S(1)}, bf16[1,1536,1024]{2,1,0:T(8,128)(2,1)}, u32[]{:S(2)}) %copy-start) | copy-done | bytes 3145752
  22.7 4.3 %products.1 = (f32[1024,512]{1,0:T(8,128)S(1)}, f32[512,512]{1,0:T(8,128)S(1)}) custom-call(bf16[1536,1024]{1,0:T(8,128)(2,1)S(1)} %bitcast.9, bf16[1536,512]{1,0:T(8,128)(2,1)S(1)} %bitcast.8, bf16[1024,512]{1,0:T(8,128)(2,1)S(1)} %compare_convert_fusion.pick_ref, f32[512,1]{1,0:T(8,128)S(1)} %copy.6.diag_ref), custom_call_target="tpu_custom_call" | custom-call | tf_op jit(solution)/shard_map/products/pallas_call | solution.py:381
  27.0 75.8 %reduce_and_share.1 = (f32[32,512]{1,0:T(8,128)S(1)}, f32[16,2,16,512]{3,2,1,0:T(8,128)S(1)}) custom-call(f32[16,2,32,512]{3,2,1,0:T(8,128)S(1)} %bitcast.10, f32[16,2,16,512]{3,2,1,0:T(8,128)S(1)} %bitcast.11, f32[32,512]{1,0:T(8,128)S(1)} %get-tuple-element.13.diag_ref), custom_call_target="tpu_custom_call" | custom-call | tf_op jit(solution)/shard_map/reduce_and_share/pallas_call | solution.py:261
  102.7 12.8 %eliminate.1 = (f32[32,1,256]{2,1,0:T(1,128)}, f32[32,1,256]{2,1,0:T(1,128)}) custom-call(f32[32,512]{1,0:T(8,128)S(1)} %get-tuple-element.14.both_ref, f32[512,512]{1,0:T(8,128)S(1)} %bitcast.12), custom_call_target="tpu_custom_call" | custom-call | tf_op jit(solution)/shard_map/eliminate/pallas_call | solution.py:340
  (2 shorter events, 0.0 us)
Async XLA Ops:
  2.4 0.9 copy-start.1
  20.8 1.9 %copy-start = (bf16[1,1536,1024]{2,1,0:T(8,128)(2,1)S(1)}, bf16[1,1536,1024]{2,1,0:T(8,128)(2,1)}, u32[]{:S(2)}) copy-start(bf16[1,1536,1024]{2,1,0:T(8,128)(2,1)} %param.4) | copy-start | bytes 9437188
